TPU v7x, 256 devices: a whole 4x4x8 slice. The times are simulated.
256 devices in a mesh: layer: 64 (over y, x_lo, z), feat: 4 (over x_hi, core).
Axes of the slice: x: 4 (x_hi: 2, x_lo: 2; x = x_hi * 2 + x_lo), y: 4, z: 8, core: 2. Of those that a mesh axis runs over, the one named last changes fastest.
Arguments:
- sources: bfloat16 [256, 8192], P(('layer', 'feat')), may hold values from -6 to 6
- targets: bfloat16 [256, 16384], P(('layer', 'feat')), may hold values from -16 to 16
- enc_weight: bfloat16 [8192, 32768], P(None, ('feat', 'layer')), may hold values from -0.0625 to 0.0625
- enc_bias: float32 [32768], P(('feat', 'layer')), may hold values from -3 to 3
- dec_weight: bfloat16 [32768, 16384], P('feat', 'layer'), may hold values from -0.03125 to 0.03125
- dec_bias: float32 [16384], P('layer'), may hold values from -3 to 3
Outputs:
- enc_grad: bfloat16 [8192, 32768], P(None, ('feat', 'layer'))
- dec_grad: bfloat16 [32768, 16384], P('feat', 'layer')
- mse: float32 [], replicated
All inputs are finite; a program needn't handle non-finite values.
Results may differ from a plain program's by a relative error of at most 0.011.
Values may be sent and summed in bfloat16 or wider, within the bound.
No kernel may reach another device: no remote copies, remote signals or barrier semaphores. Data moves between devices by JAX's collectives and lax.ppermute only.
A program may use at most 128 MiB of HBM per device.

v0:
```python
import math
import jax
import jax.numpy as jnp
from jax import lax
from jax.sharding import PartitionSpec as P


def per_device(sources, targets, enc_weight, enc_bias, dec_weight, dec_bias):
    inputs = lax.all_gather(sources, ("layer", "feat"), axis=0, tiled=True)
    tokens = inputs.shape[0]
    preact = jnp.dot(inputs, enc_weight, preferred_element_type=jnp.float32) + enc_bias
    feats = jax.nn.gelu(preact).astype(jnp.bfloat16)
    n_layer = lax.axis_size("layer")
    width = dec_weight.shape[1]
    spread = lax.all_gather(targets, "feat", axis=0, tiled=True)
    blocks = spread.reshape(spread.shape[0], n_layer, width)
    owned = lax.all_to_all(blocks, "layer", split_axis=1, concat_axis=0, tiled=True)
    wanted = owned.reshape(tokens, width)
    all_feats = lax.all_gather(feats, "layer", axis=1, tiled=True)
    partial_value = jnp.dot(all_feats, dec_weight, preferred_element_type=jnp.float32)
    factor = 1.0 / math.sqrt(tokens)
    outputs = lax.psum(partial_value.astype(jnp.bfloat16), "feat").astype(jnp.float32) + dec_bias
    misfit = outputs - wanted.astype(jnp.float32)
    errors = (misfit * factor).astype(jnp.bfloat16)
    total_sq = lax.psum(jnp.sum(misfit * misfit), "layer")
    mse = total_sq / (tokens * n_layer * width)
    dec_grad = lax.dot_general(
        all_feats, errors, (((0,), (0,)), ((), ())), preferred_element_type=jnp.float32
    ).astype(jnp.bfloat16)
    grad_rows = lax.psum_scatter(
        lax.dot_general(
            dec_weight, errors, (((1,), (1,)), ((), ())), preferred_element_type=jnp.float32
        ),
        "layer",
        scatter_dimension=0,
        tiled=True,
    )
    feat_grad = grad_rows.T
    _, pullback = jax.vjp(jax.nn.gelu, preact)
    pre_grad = pullback(feat_grad)[0].astype(jnp.bfloat16)
    enc_grad = lax.dot_general(
        inputs, pre_grad, (((0,), (0,)), ((), ())), preferred_element_type=jnp.float32
    ).astype(jnp.bfloat16)
    return (enc_grad, dec_grad, mse)


def solution(mesh):
    return jax.shard_map(
        per_device,
        mesh=mesh,
        in_specs=(
            P(("layer", "feat"), None),
            P(("layer", "feat"), None),
            P(None, ("feat", "layer")),
            P(("feat", "layer")),
            P("feat", "layer"),
            P("layer"),
        ),
        out_specs=(P(None, ("feat", "layer")), P("feat", "layer"), P()),
        check_vma=False,
    )
```

profile of v0, /device:TPU:4, one launch (start us, length us, event | category | flops | bytes accessed | tf_op | source)
XLA Modules:
  0.0 1093.3 jit_solution(547445359311050839)
XLA Ops:
  7.2 0.0 copy-start
  7.2 0.0 copy-start.1
  7.2 0.0 all-gather.7.cloned.1.call-start
  7.2 0.7 all-gather.7.cloned.1.call-update
  7.9 0.0 all-gather.5.cloned.1.call-start
  8.0 423.7 %all-gather.7.cloned.1.call-done = bf16[256,1,8192]{2,1,0:T(2,128)(2,1)} async-done(((bf16[1,1,8192]{2,1,0:T(2,128)(2,1)}), bf16[256,1,8192]{2,1,0:T(2,128)(2,1)}) %all-gather.7.cloned.1.call-update) | async-done | bytes 4194320 | tf_op jit(solution)/shard_map/all_gather | solution.py:9
  431.6 0.0 copy-done
  431.6 8.9 multiply_convert_fusion.1
  440.6 0.0 all-gather.5.cloned.1.call-update
  440.6 0.0 copy-done.1
  440.6 7.3 all-gather.1
  447.9 1.5 reduce
  449.3 7.6 all-to-all-start
  457.0 0.0 copy-start.2
  457.0 0.0 all-reduce.2.cloned.1.call-start
  457.0 224.1 %all-gather.5.cloned.1.call-done = bf16[256,8192]{1,0:T(8,128)(2,1)} async-done(((bf16[256,128]{1,0:T(8,128)(2,1)}), bf16[256,8192]{1,0:T(8,128)(2,1)}) %all-gather.5.cloned.1.call-update) | async-done | bytes 4194320 | tf_op jit(solution)/shard_map/all_gather | solution.py:19
  681.1 5.4 convolution_convert_fusion.2
  686.5 0.0 all-reduce.2.cloned.1.call-update
  686.5 0.0 reduce-scatter.2.cloned.1.call-start
  686.6 0.0 all-to-all-done
  686.6 0.1 reshape.18
  686.7 40.1 %all-reduce.2.cloned.1.call-done = bf16[256,256]{1,0:T(8,128)(2,1)} async-done(((bf16[256,256]{1,0:T(8,128)(2,1)}), bf16[256,256]{1,0:T(8,128)(2,1)}) %all-reduce.2.cloned.1.call-update) | async-done | bytes 131088 | tf_op jit(solution)/shard_map/psum | solution.py:22
  726.8 0.0 copy-done.2
  726.8 1.6 multiply_reduce_fusion
  728.4 6.7 convolution_bitcast_fusion
  735.1 0.0 reduce-scatter.2.cloned.1.call-update
  735.1 160.3 %psum.15 = f32[]{:T(128)} all-reduce(f32[]{:T(128)} %get-tuple-element.12), channel_id=1, replica_groups=mesh['layer'=64,'feat'=4] {'layer'}, use_global_device_ids=true, to_apply=%region_3.0 | all-reduce | flops 1 | bytes 8 | tf_op jit(solution)/shard_map/psum | solution.py:25
  896.1 5.5 convolution_convert_fusion
  901.7 170.2 %reduce-scatter.2.cloned.1.call-done = f32[128,256]{0,1:T(8,128)} async-done(((f32[8192,256]{0,1:T(8,128)}), f32[128,256]{0,1:T(8,128)}) %reduce-scatter.2.cloned.1.call-update) | async-done | bytes 131088 | tf_op jit(solution)/shard_map/reduce_scatter | solution.py:30
  1071.8 9.8 fusion
  1081.6 4.1 copy.13
  (1 shorter events, 0.0 us)
Async XLA Ops:
  7.2 424.5 %copy-start = (bf16[8192,128]{1,0:T(8,128)(2,1)S(1)}, bf16[8192,128]{1,0:T(8,128)(2,1)}, u32[]{:S(2)}) copy-start(bf16[8192,128]{1,0:T(8,128)(2,1)} %param.8) | copy-start | bytes 6291460
  7.2 433.4 %copy-start.1 = (bf16[1,16384]{1,0:T(2,128)(2,1)S(1)}, bf16[1,16384]{1,0:T(2,128)(2,1)}, u32[]{:S(2)}) copy-start(bf16[1,16384]{1,0:T(2,128)(2,1)} %param.7) | copy-start | bytes 98308
  7.2 424.4 %all-gather.7.cloned.1.call-start = ((), (), s32[]{:S(2)}) async-start(), calls=%async_computation.5 | async-start | bytes 8421376 | tf_op jit(solution)/shard_map/all_gather | solution.py:9
  7.9 673.2 %all-gather.5.cloned.1.call-start = ((), (), s32[]{:S(2)}) async-start(), calls=%async_computation.2 | async-start | bytes 4259840 | tf_op jit(solution)/shard_map/all_gather | solution.py:19
  449.3 237.3 %all-to-all-start = ((bf16[4,64,256]{2,0,1:T(4,128)(2,1)}), bf16[4,64,256]{2,0,1:T(4,128)(2,1)S(1)}, u32[]{:S(2)}, u32[]{:S(2)}) async-start(bf16[4,64,256]{2,0,1:T(4,128)(2,1)} %bitcast.9), calls=%async_computation | async-start | bytes 262144 | tf_op jit(solution)/shard_map/all_to_all | solution.py:17
  457.0 269.9 %copy-start.2 = (f32[256]{0:T(256)S(1)}, f32[256]{0:T(256)}, u32[]{:S(2)}) copy-start(f32[256]{0:T(256)} %param.11) | copy-start | bytes 3076
  457.0 269.8 %all-reduce.2.cloned.1.call-start = ((), (), s32[]{:S(2)}) async-start(), calls=%async_computation.3 | async-start | bytes 262144 | tf_op jit(solution)/shard_map/psum | solution.py:22
  686.5 385.3 %reduce-scatter.2.cloned.1.call-start = ((), (), s32[]{:S(2)}) async-start(), calls=%async_computation.4 | async-start | bytes 8519680 | tf_op jit(solution)/shard_map/reduce_scatter | solution.py:30
Sparse Core Ops, SparseCore 0:
  9.9 421.7 all-gather.6
  440.7 240.4 all-gather.4
  686.7 40.1 all-reduce.1
  735.3 336.4 reduce-scatter.1
where the time goes:
time: 1090 us
  waiting for transfers between devices  859 us (79%)
  blocking collectives  168 us (15%)
  matrix products  36.3 us (3%)
  between operations  15.6 us (1%)
    all_gather x1, waiting for transfers between devices, per_device(): inputs = lax.all_gather(sources, ('layer', 'feat'), axis=0, tiled=True)  424 us
    all_gather x1, waiting for transfers between devices, per_device(): all_feats = lax.all_gather(feats, 'layer', axis=1, tiled=True)  224 us
    reduce_scatter x1, waiting for transfers between devices, per_device(): lax.psum_scatter(lax.dot_general(dec_weight, errors, (((1,), (1,)), ((),...  170 us
    psum x1, blocking collectives, per_device(): total_sq = lax.psum(jnp.sum(misfit * misfit), 'layer')  160 us
    psum x1, waiting for transfers between devices, per_device(): lax.psum(partial_value.astype(jnp.bfloat16), 'feat').astype(jnp.float32)  40.1 us
  transfers between devices with their start and end apart: 5, of which 4 were waited for; matrix products, arithmetic and copies ran while one was open for 1% of the time, Pallas kernels for 0%

commit v1 on v0

--- a/solution.py
+++ b/solution.py
@@ -16,7 +16,9 @@
     blocks = spread.reshape(spread.shape[0], n_layer, width)
     owned = lax.all_to_all(blocks, "layer", split_axis=1, concat_axis=0, tiled=True)
     wanted = owned.reshape(tokens, width)
-    all_feats = lax.all_gather(feats, "layer", axis=1, tiled=True)
+    all_feats = jnp.concatenate(
+        lax.all_to_all(jnp.stack([feats] * lax.axis_size("layer")), "layer", 0, 0), axis=1
+    )
     partial_value = jnp.dot(all_feats, dec_weight, preferred_element_type=jnp.float32)
     factor = 1.0 / math.sqrt(tokens)
     outputs = lax.psum(partial_value.astype(jnp.bfloat16), "feat").astype(jnp.float32) + dec_bias

time: 1090 us -> 967 us (0.89)
  waiting for transfers between devices: 859 us -> 717 us
    all_gather x1 -> x0, waiting for transfers between devices: 224 us -> none  [per_device(): all_feats = lax.all_gather(feats, 'layer', axis=1, tiled=True)]
    all_to_all x0 -> x1, waiting for transfers between devices: none -> 78.6 us  [per_device(): lax.all_to_all(jnp.stack([feats] * lax.axis_size('layer')), 'layer', 0, 0)]
  transfers between devices with their start and end apart: 5 -> 5, of which waited for: 4 -> 5; matrix products, arithmetic and copies ran while one was open for 1% -> 1% of each run, Pallas kernels for 0% -> 0%
where the time goes in v1:
time: 967 us
  waiting for transfers between devices  717 us (74%)
  blocking collectives  173 us (18%)
  matrix products  35.7 us (4%)
  between operations  15.6 us (2%)
  starting transfers between devices  15.5 us (2%)
    all_gather x1, waiting for transfers between devices, per_device(): inputs = lax.all_gather(sources, ('layer', 'feat'), axis=0, tiled=True)  424 us
    reduce_scatter x1, waiting for transfers between devices, per_device(): lax.psum_scatter(lax.dot_general(dec_weight, errors, (((1,), (1,)), ((),...  170 us
    psum x1, blocking collectives, per_device(): total_sq = lax.psum(jnp.sum(misfit * misfit), 'layer')  160 us
    all_to_all x1, waiting for transfers between devices, per_device(): lax.all_to_all(jnp.stack([feats] * lax.axis_size('layer')), 'layer', 0, 0)  78.6 us
    psum x1, waiting for transfers between devices, per_device(): lax.psum(partial_value.astype(jnp.bfloat16), 'feat').astype(jnp.float32)  38.4 us
  transfers between devices with their start and end apart: 5, of which 5 were waited for; matrix products, arithmetic and copies ran while one was open for 1% of the time, Pallas kernels for 0%

profile of v1, /device:TPU:4, one launch (start us, length us, event | category | flops | bytes accessed | tf_op | source)
XLA Modules:
  0.0 966.6 jit_solution(5997116779071456082)
XLA Ops:
  7.2 0.0 copy-start
  7.2 0.0 all-gather.4.cloned.1.call-start
  7.2 0.7 all-gather.4.cloned.1.call-update
  7.9 423.7 %all-gather.4.cloned.1.call-done = bf16[256,1,8192]{2,1,0:T(2,128)(2,1)} async-done(((bf16[1,1,8192]{2,1,0:T(2,128)(2,1)}), bf16[256,1,8192]{2,1,0:T(2,128)(2,1)}) %all-gather.4.cloned.1.call-update) | async-done | bytes 4194320 | tf_op jit(solution)/shard_map/all_gather | solution.py:9
  431.6 0.0 copy-done
  431.6 8.3 multiply_convert_fusion.1
  439.9 0.1 copy.13
  440.0 2.5 stack.2
  442.5 0.0 copy-start.1
  442.5 8.0 all-to-all-start
  450.6 0.0 copy-done.1
  450.6 12.4 %all-gather.1 = bf16[4,1,16384]{2,1,0:T(2,128)(2,1)S(1)} all-gather(bf16[1,1,16384]{2,1,0:T(2,128)(2,1)S(1)} %bitcast.47), channel_id=1, replica_groups=mesh['layer'=64,'feat'=4] {'feat'}, dimensions={0}, use_global_device_ids=true | all-gather | bytes 163840 | tf_op jit(solution)/shard_map/all_gather | solution.py:15
  463.0 1.5 reduce
  464.4 78.6 %all-to-all-done = bf16[64,256,128]{1,2,0:T(8,128)(2,1)} async-done(((bf16[64,256,128]{1,2,0:T(8,128)(2,1)}), bf16[64,256,128]{1,2,0:T(8,128)(2,1)}, u32[]{:S(2)}, u32[]{:S(2)}) %all-to-all-start) | async-done | bytes 4194336 | tf_op jit(solution)/shard_map/all_to_all | solution.py:20
  543.0 7.4 all-to-all-start.1
  550.4 0.0 all-reduce.2.cloned.1.call-start
  550.4 0.0 copy-start.2
  550.5 5.4 convolution_convert_fusion.2
  555.9 0.0 all-reduce.2.cloned.1.call-update
  555.9 0.0 reduce-scatter.2.cloned.1.call-start
  556.0 5.6 all-to-all-done.1
  561.6 0.1 reshape.28
  561.7 38.4 %all-reduce.2.cloned.1.call-done = bf16[256,256]{1,0:T(8,128)(2,1)} async-done(((bf16[256,256]{1,0:T(8,128)(2,1)}), bf16[256,256]{1,0:T(8,128)(2,1)}) %all-reduce.2.cloned.1.call-update) | async-done | bytes 131088 | tf_op jit(solution)/shard_map/psum | solution.py:24
  600.1 0.0 copy-done.2
  600.1 1.6 multiply_reduce_fusion
  601.7 6.7 convolution_bitcast_fusion
  608.4 0.0 reduce-scatter.2.cloned.1.call-update
  608.4 160.3 %psum.15 = f32[]{:T(128)} all-reduce(f32[]{:T(128)} %get-tuple-element.12), channel_id=1, replica_groups=mesh['layer'=64,'feat'=4] {'layer'}, use_global_device_ids=true, to_apply=%region_3.0 | all-reduce | flops 1 | bytes 8 | tf_op jit(solution)/shard_map/psum | solution.py:27
  769.4 5.5 convolution_convert_fusion
  774.8 170.3 %reduce-scatter.2.cloned.1.call-done = f32[128,256]{0,1:T(8,128)} async-done(((f32[8192,256]{0,1:T(8,128)}), f32[128,256]{0,1:T(8,128)}) %reduce-scatter.2.cloned.1.call-update) | async-done | bytes 131088 | tf_op jit(solution)/shard_map/reduce_scatter | solution.py:32
  945.1 9.8 %fusion = bf16[8192,128]{0,1:T(8,128)(2,1)} fusion(bf16[256,1,8192]{2,1,0:T(2,128)(2,1)} %all-gather.4.cloned.1.call-done, f32[256,128]{1,0:T(8,128)S(1)} %get-tuple-element.15, f32[128,256]{0,1:T(8,128)} %reduce-scatter.2.cloned.1.call-done), kind=kOutput, calls=%fused_computation.3 | convolution fusion | flops 538574848 | bytes 6553600 | tf_op jit(solution)/shard_map/dot_general | solution.py:43
  954.9 4.1 copy.15
  (1 shorter events, 0.0 us)
Async XLA Ops:
  7.2 424.5 %copy-start = (bf16[8192,128]{1,0:T(8,128)(2,1)S(1)}, bf16[8192,128]{1,0:T(8,128)(2,1)}, u32[]{:S(2)}) copy-start(bf16[8192,128]{1,0:T(8,128)(2,1)} %param.8) | copy-start | bytes 6291460
  7.2 424.4 %all-gather.4.cloned.1.call-start = ((), (), s32[]{:S(2)}) async-start(), calls=%async_computation.5 | async-start | bytes 8421376 | tf_op jit(solution)/shard_map/all_gather | solution.py:9
  442.5 8.0 copy-start.1
  442.5 100.5 %all-to-all-start = ((bf16[64,256,128]{1,2,0:T(8,128)(2,1)}), bf16[64,256,128]{1,2,0:T(8,128)(2,1)}, u32[]{:S(2)}, u32[]{:S(2)}) async-start(bf16[64,256,128]{1,2,0:T(8,128)(2,1)} %stack.2), calls=%async_computation | async-start | bytes 8388608 | tf_op jit(solution)/shard_map/all_to_all | solution.py:20
  543.0 18.5 %all-to-all-start.1 = ((bf16[4,64,256]{2,0,1:T(4,128)(2,1)}), bf16[4,64,256]{2,0,1:T(4,128)(2,1)S(1)}, u32[]{:S(2)}, u32[]{:S(2)}) async-start(bf16[4,64,256]{2,0,1:T(4,128)(2,1)} %bitcast.12), calls=%async_computation.1 | async-start | bytes 262144 | tf_op jit(solution)/shard_map/all_to_all | solution.py:17
  550.4 49.7 %all-reduce.2.cloned.1.call-start = ((), (), s32[]{:S(2)}) async-start(), calls=%async_computation.3 | async-start | bytes 262144 | tf_op jit(solution)/shard_map/psum | solution.py:24
  550.4 49.6 %copy-start.2 = (f32[256]{0:T(256)S(1)}, f32[256]{0:T(256)}, u32[]{:S(2)}) copy-start(f32[256]{0:T(256)} %param.11) | copy-start | bytes 3076
  555.9 389.2 %reduce-scatter.2.cloned.1.call-start = ((), (), s32[]{:S(2)}) async-start(), calls=%async_computation.4 | async-start | bytes 8519680 | tf_op jit(solution)/shard_map/reduce_scatter | solution.py:32
Sparse Core Ops, SparseCore 0:
  9.9 421.7 all-gather.3
  556.0 44.0 all-reduce.1
  608.5 336.5 reduce-scatter.1
